TPU v7x, 256 devices: a whole 4x4x8 slice. The times are simulated.
256 devices in a mesh: seq: 8 (over y, core), chan: 32 (over z, x).
Axes of the slice: x: 4, y: 4, z: 8, core: 2. Of those that a mesh axis runs over, the one named last changes fastest.
Arguments:
- tokens: bfloat16 [1024, 4096], P('seq', 'chan'), may hold values from -6 to 6
- in_weight: bfloat16 [4096, 3, 4096], P(None, None, 'chan'), may hold values from -0.09375 to 0.09375
- short_kernel: float32 [3, 3, 4096], P(None, None, 'chan'), may hold values from -3 to 3
- filters: float32 [2, 1024, 4096], P(None, 'seq', 'chan'), may hold values from -0.5 to 0.5
- skip_gain: float32 [2, 4096], P(None, 'chan'), may hold values from 0.5 to 1.5
- out_weight: bfloat16 [4096, 4096], P('chan'), may hold values from -0.09375 to 0.09375
- cotangent: bfloat16 [1024, 4096], P('seq', 'chan'), may hold values from -6 to 6
Outputs:
- mixed: bfloat16 [1024, 4096], P('seq', 'chan')
- token_grad: bfloat16 [1024, 4096], P('seq', 'chan')
All inputs are finite; a program needn't handle non-finite values.
Results may differ from a plain program's by a relative error of at most 0.0049.
Values may be sent and summed in bfloat16 or wider, within the bound.
No kernel may reach another device: no remote copies, remote signals or barrier semaphores. Data moves between devices by JAX's collectives and lax.ppermute only.
A program may use at most 64 MiB of HBM per device.

v0:
```python
import math
import jax
import jax.numpy as jnp
from jax import lax
from jax.sharding import PartitionSpec as P

PRECISE = lax.Precision.HIGHEST


def swapped(value, axis, apart):
    mask = 2**apart
    pairs = [(source, source ^ mask) for source in range(lax.axis_size(axis))]
    return lax.ppermute(value, axis, pairs)


def passed_along(value, axis, steps):
    count = lax.axis_size(axis)
    first, last = (max(0, -steps), min(count, count - steps))
    return lax.ppermute(value, axis, [(source, source + steps) for source in range(first, last)])


def rotate(real_part, imag_part, turn_angle):
    cosine = jnp.cos(turn_angle)
    sine_part = jnp.sin(turn_angle)
    return (real_part * cosine - imag_part * sine_part, real_part * sine_part + imag_part * cosine)


def block_dft(real_part, imag_part, flip_sign):
    full_shape = real_part.shape
    length = full_shape[-2]
    token_positions = jnp.arange(length, dtype=jnp.int32)
    table_angle = (
        2.0
        * math.pi
        / length
        * (token_positions[:, None] * token_positions[None, :] % length).astype(jnp.float32)
    )
    cosine = jnp.cos(table_angle)
    sine_part = flip_sign * jnp.sin(table_angle)
    summed = cosine + sine_part
    differ = sine_part - cosine
    flat_re = real_part.reshape((-1, length, full_shape[-1]))
    flat_im = imag_part.reshape((-1, length, full_shape[-1]))
    product_one = jnp.einsum("kn,anc->akc", cosine, flat_re + flat_im, precision=PRECISE)
    product_two = jnp.einsum("kn,anc->akc", summed, flat_im, precision=PRECISE)
    product_three = jnp.einsum("kn,anc->akc", differ, flat_re, precision=PRECISE)
    return (
        (product_one - product_two).reshape(full_shape),
        (product_one + product_three).reshape(full_shape),
    )


def twiddle(real_part, imag_part, column, full_length, flip_sign):
    row_ids = jnp.arange(real_part.shape[-2], dtype=jnp.int32)[:, None]
    turn_angle = (
        flip_sign
        * 2.0
        * math.pi
        / full_length
        * (column * row_ids % full_length).astype(jnp.float32)
    )
    return rotate(real_part, imag_part, turn_angle)


def reversed_index(seq_index, levels):
    flipped = jnp.zeros((), jnp.int32)
    for section_bit in range(levels):
        flipped = flipped + seq_index // 2**section_bit % 2 * 2 ** (levels - 1 - section_bit)
    return flipped


def spectrum(signal):
    seq_count = lax.axis_size("seq")
    levels = seq_count.bit_length() - 1
    seq_index = lax.axis_index("seq")
    blocks = signal.shape[1]
    full_length = 2 * seq_count * blocks
    quarter = jnp.arange(2, dtype=jnp.int32)
    lift_angle = -math.pi / seq_count * seq_index.astype(jnp.float32)
    real_part = jnp.stack([signal, signal * jnp.cos(lift_angle)])
    imag_part = jnp.stack([jnp.zeros_like(signal), signal * jnp.sin(lift_angle)])
    for section_bit in reversed(range(levels)):
        half_span = 2**section_bit
        other_re, other_im = swapped((real_part, imag_part), "seq", section_bit)
        is_upper = seq_index // half_span % 2 == 1
        phase_angle = -math.pi / half_span * (seq_index % half_span).astype(jnp.float32)
        diff_re, diff_im = rotate(other_re - real_part, other_im - imag_part, phase_angle)
        real_part = jnp.where(is_upper, diff_re, real_part + other_re)
        imag_part = jnp.where(is_upper, diff_im, imag_part + other_im)
    column = 2 * reversed_index(seq_index, levels) + quarter[:, None, None, None]
    real_part, imag_part = twiddle(real_part, imag_part, column, full_length, -1.0)
    return block_dft(real_part, imag_part, -1.0)


def restore(real_part, imag_part):
    seq_count = lax.axis_size("seq")
    levels = seq_count.bit_length() - 1
    seq_index = lax.axis_index("seq")
    blocks = real_part.shape[-2]
    full_length = 2 * seq_count * blocks
    quarter = jnp.arange(2, dtype=jnp.int32)
    real_part, imag_part = block_dft(real_part, imag_part, 1.0)
    real_part = real_part / blocks
    imag_part = imag_part / blocks
    column = 2 * reversed_index(seq_index, levels) + quarter[:, None, None, None]
    real_part, imag_part = twiddle(real_part, imag_part, column, full_length, 1.0)
    for section_bit in range(levels):
        half_span = 2**section_bit
        other_re, other_im = swapped((real_part, imag_part), "seq", section_bit)
        is_upper = seq_index // half_span % 2 == 1
        phase_angle = math.pi / half_span * (seq_index % half_span).astype(jnp.float32)
        turned_re, turned_im = rotate(other_re, other_im, phase_angle)
        local_rotated_real, own_turn_im = rotate(real_part, imag_part, phase_angle)
        new_re = jnp.where(is_upper, other_re - local_rotated_real, real_part + turned_re)
        new_im = jnp.where(is_upper, other_im - own_turn_im, imag_part + turned_im)
        real_part = 0.5 * new_re
        imag_part = 0.5 * new_im
    lift_angle = math.pi / seq_count * seq_index.astype(jnp.float32)
    return 0.5 * (
        real_part[0] + real_part[1] * jnp.cos(lift_angle) - imag_part[1] * jnp.sin(lift_angle)
    )


def product_of(left_pair, right_pair, conjugate):
    left_re, left_im = left_pair
    right_re, right_im = right_pair
    if conjugate:
        right_im = -right_im
    return (left_re * right_re - left_im * right_im, left_re * right_im + left_im * right_re)


def select_entry(pair, entry):
    return (pair[0][:, entry : entry + 1], pair[1][:, entry : entry + 1])


def on_device(tokens, in_weight, short_kernel, filters, skip_gain, out_weight, cotangent):
    chans = in_weight.shape[2]
    width = in_weight.shape[0]
    blocks = tokens.shape[0]
    flat_in = in_weight.reshape((width, 3 * chans))
    projected = jnp.dot(
        lax.all_gather(tokens, "chan", axis=1, tiled=True),
        flat_in,
        preferred_element_type=jnp.float32,
    )
    projected = projected.reshape((blocks, 3, chans))
    taps = short_kernel.shape[0]
    prior = passed_along(projected[blocks - (taps - 1) :], "seq", 1)
    padded = jnp.concatenate([prior, projected], axis=0)
    shorted = short_kernel[0] * projected
    for tap_index in range(1, taps):
        offset = taps - 1 - tap_index
        shorted = shorted + short_kernel[tap_index] * padded[offset : offset + blocks]
    values = shorted[:, 0]
    gate_one = shorted[:, 1]
    gate_two = shorted[:, 2]
    spectra = spectrum(jnp.stack([filters[0], filters[1], values]))
    conv_one = (
        restore(*product_of(select_entry(spectra, 2), select_entry(spectra, 0), False))[0]
        + skip_gain[0] * values
    )
    first_out = gate_one * conv_one
    first_spec = spectrum(first_out[None])
    conv_two = (
        restore(*product_of(first_spec, select_entry(spectra, 1), False))[0]
        + skip_gain[1] * first_out
    )
    second_order_output = (gate_two * conv_two).astype(jnp.bfloat16)
    picked = out_weight
    mixed = lax.psum_scatter(
        lax.dot_general(
            picked,
            second_order_output,
            (((0,), (1,)), ((), ())),
            preferred_element_type=jnp.float32,
        ),
        "chan",
        scatter_dimension=0,
        tiled=True,
    ).T.astype(jnp.bfloat16)
    grad_two = lax.dot_general(
        lax.all_gather(cotangent, "chan", axis=1, tiled=True),
        out_weight,
        (((1,), (1,)), ((), ())),
        preferred_element_type=jnp.float32,
    )
    grad_gate_two = grad_two * conv_two
    grad_conv_two = grad_two * gate_two
    grad_spec = spectrum(grad_conv_two[None])
    grad_first = (
        restore(*product_of(grad_spec, select_entry(spectra, 1), True))[0]
        + skip_gain[1] * grad_conv_two
    )
    first_gate_gradient = grad_first * conv_one
    grad_conv_one = grad_first * gate_one
    inner_spec = spectrum(grad_conv_one[None])
    grad_values = (
        restore(*product_of(inner_spec, select_entry(spectra, 0), True))[0]
        + skip_gain[0] * grad_conv_one
    )
    grad_short = jnp.stack([grad_values, first_gate_gradient, grad_gate_two], axis=1)
    later = passed_along(grad_short[: taps - 1], "seq", -1)
    padded_grad = jnp.concatenate([grad_short, later], axis=0)
    grad_proj = short_kernel[0] * grad_short
    for tap_index in range(1, taps):
        grad_proj = (
            grad_proj + short_kernel[tap_index] * padded_grad[tap_index : tap_index + blocks]
        )
    grad_proj = grad_proj.astype(jnp.bfloat16)
    grad_flat = grad_proj.reshape((blocks, 3 * chans))
    picked = flat_in
    token_grad = lax.psum_scatter(
        lax.dot_general(
            picked, grad_flat, (((1,), (1,)), ((), ())), preferred_element_type=jnp.float32
        ),
        "chan",
        scatter_dimension=0,
        tiled=True,
    ).T.astype(jnp.bfloat16)
    return (mixed, token_grad)


def solution(mesh):
    in_specs = (
        P("seq", "chan"),
        P(None, None, "chan"),
        P(None, None, "chan"),
        P(None, "seq", "chan"),
        P(None, "chan"),
        P("chan", None),
        P("seq", "chan"),
    )
    out_specs = (P("seq", "chan"), P("seq", "chan"))
    return jax.shard_map(
        on_device, mesh=mesh, in_specs=in_specs, out_specs=out_specs, check_vma=False
    )
```

profile of v0, /device:TPU:8, one launch (start us, length us, event | category | flops | bytes accessed | tf_op | source)
XLA Modules:
  0.0 760.7 jit_solution(1646638522925081413)
XLA Ops:
  8.9 4.8 copy.188
  13.7 70.3 %all-gather.3.cloned.1.call-done = bf16[128,4096]{1,0:T(8,128)(2,1)} async-done(((bf16[128,128]{1,0:T(8,128)(2,1)}), bf16[128,4096]{1,0:T(8,128)(2,1)}) %all-gather.3.cloned.1.call-update) | async-done | bytes 1048592 | tf_op jit(solution)/shard_map/all_gather | solution.py:142
  84.0 3.3 fusion.349
  87.3 1.9 collective-permute-start
  89.3 66.9 %all-gather.5.cloned.1.call-done = bf16[128,4096]{1,0:T(8,128)(2,1)} async-done(((bf16[128,128]{1,0:T(8,128)(2,1)}), bf16[128,4096]{1,0:T(8,128)(2,1)}) %all-gather.5.cloned.1.call-update) | async-done | bytes 1048592 | tf_op jit(solution)/shard_map/all_gather | solution.py:182
  156.2 1.7 fusion.350
  158.3 2.2 collective-permute-start.1
  160.6 1.5 collective-permute-start.2
  162.1 2.2 collective-permute-start.25
  164.3 1.5 collective-permute-start.26
  166.2 13.1 %collective-permute-done.25 = f32[2,1,128,128]{3,2,1,0:T(8,128)S(1)} collective-permute-done((f32[2,1,128,128]{3,2,1,0:T(8,128)S(1)}, f32[2,1,128,128]{3,2,1,0:T(8,128)S(1)}, u32[]{:S(2)}, u32[]{:S(2)}) %collective-permute-start.25) | collective-permute-done | bytes 131104 | tf_op jit(solution)/shard_map/ppermute | solution.py:13
  179.3 2.8 collective-permute-done.26
  182.7 1.5 collective-permute-start.28
  186.1 1.5 collective-permute-start.4
  188.6 2.8 collective-permute-done.28
  192.1 6.9 collective-permute-done.3
  198.9 4.2 collective-permute-done.4
  215.7 3.8 collective-permute-done.33
  219.6 2.0 collective-permute-done.34
  222.1 3.3 collective-permute-start.36
  225.3 4.1 collective-permute-done.35
  232.1 2.7 collective-permute-start.38
  234.7 3.2 collective-permute-done.37
  241.8 2.6 collective-permute-done.39
  255.2 4.3 collective-permute-done.10
  259.5 2.0 collective-permute-done.9
  261.6 2.4 collective-permute-start.11
  265.3 3.9 collective-permute-done.11
  269.1 1.8 collective-permute-done.12
  271.1 2.2 collective-permute-start.13
  273.4 1.5 collective-permute-start.14
  274.9 3.8 collective-permute-done.13
  282.9 2.4 collective-permute-done.15
  296.7 4.3 collective-permute-done.21
  301.0 2.0 collective-permute-done.22
  303.1 1.9 collective-permute-start.23
  305.1 1.7 collective-permute-start.24
  306.7 4.3 collective-permute-done.23
  312.6 1.7 convolution_bitcast_fusion.1
  318.2 4.3 collective-permute-done.45
  322.6 2.2 collective-permute-done.46
  324.8 1.8 collective-permute-start.47
  326.6 1.8 collective-permute-start.48
  328.5 4.3 collective-permute-done.47
  334.3 1.9 collective-permute-start.49
  337.5 2.5 convolution_bitcast_fusion
  340.0 191.7 %reduce-scatter.3.cloned.1.call-done = f32[128,128]{0,1:T(8,128)} async-done(((f32[4096,128]{0,1:T(8,128)}), f32[128,128]{0,1:T(8,128)}) %reduce-scatter.3.cloned.1.call-update) | async-done | bytes 65552 | tf_op jit(solution)/shard_map/reduce_scatter | solution.py:170
  533.2 219.3 %reduce-scatter.5.cloned.1.call-done = f32[128,128]{0,1:T(8,128)} async-done(((f32[4096,128]{0,1:T(8,128)}), f32[128,128]{0,1:T(8,128)}) %reduce-scatter.5.cloned.1.call-update) | async-done | bytes 65552 | tf_op jit(solution)/shard_map/reduce_scatter | solution.py:212
  (186 shorter events, 64.0 us)
Async XLA Ops:
  7.2 76.8 %all-gather.3.cloned.1.call-start = ((), (), s32[]{:S(2)}) async-start(), calls=%async_computation.2 | async-start | bytes 1081344 | tf_op jit(solution)/shard_map/all_gather | solution.py:142
  7.9 148.3 %all-gather.5.cloned.1.call-start = ((), (), s32[]{:S(2)}) async-start(), calls=%async_computation.4 | async-start | bytes 1081344 | tf_op jit(solution)/shard_map/all_gather | solution.py:182
  8.7 523.1 %reduce-scatter.3.cloned.1.call-start = ((), (), s32[]{:S(2)}) async-start(), calls=%async_computation.3 | async-start | bytes 2162688 | tf_op jit(solution)/shard_map/reduce_scatter | solution.py:170
  87.3 70.8 %collective-permute-start = (f32[2,3,128]{2,0,1:T(2,128)S(1)}, f32[2,3,128]{2,0,1:T(2,128)S(1)}, u32[]{:S(2)}, u32[]{:S(2)}) collective-permute-start(f32[2,3,128]{2,0,1:T(2,128)S(1)} %slice_bitcast_fusion.13), channel_id=1, source_target_pairs={{0,32},{32,64},{64,96},{96,128},{128,160},{160,192},{192,224},{1,3... | collective-permute-start | bytes 9224 | tf_op jit(solution)/shard_map/ppermute | solution.py:19
  158.3 25.9 %collective-permute-start.1 = (f32[2,3,128,128]{3,2,1,0:T(8,128)S(1)}, f32[2,3,128,128]{3,2,1,0:T(8,128)}, u32[]{:S(2)}, u32[]{:S(2)}) collective-permute-start(f32[2,3,128,128]{3,2,1,0:T(8,128)S(1)} %pad_maximum_fusion), channel_id=1, source_target_pairs={{0,128},{32,160},{64,192},{96,224},{128,0},{160,32},{192,64},{224,... | collective-permute-start | bytes 1179656 | tf_op jit(solution)/shard_map/ppermute | solution.py:13
  160.6 23.7 %collective-permute-start.2 = (f32[2,3,128,128]{3,2,1,0:T(8,128)S(1)}, f32[2,3,128,128]{3,2,1,0:T(8,128)}, u32[]{:S(2)}, u32[]{:S(2)}) collective-permute-start(f32[2,3,128,128]{3,2,1,0:T(8,128)S(1)} %stack.71), channel_id=1, source_target_pairs={{0,128},{32,160},{64,192},{96,224},{128,0},{160,32},{192,64},{224,... | collective-permute-start | bytes 1179656 | tf_op jit(solution)/shard_map/ppermute | solution.py:13
  162.1 17.2 %collective-permute-start.25 = (f32[2,1,128,128]{3,2,1,0:T(8,128)S(1)}, f32[2,1,128,128]{3,2,1,0:T(8,128)S(1)}, u32[]{:S(2)}, u32[]{:S(2)}) collective-permute-start(f32[2,1,128,128]{3,2,1,0:T(8,128)S(1)} %pad_maximum_fusion.6), channel_id=1, source_target_pairs={{0,128},{32,160},{64,192},{96,224},{128,0},{160,32},{192,64},{224,... | collective-permute-start | bytes 393224 | tf_op jit(solution)/shard_map/ppermute | solution.py:13
  164.3 17.7 %collective-permute-start.26 = (f32[2,1,128,128]{3,2,1,0:T(8,128)S(1)}, f32[2,1,128,128]{3,2,1,0:T(8,128)S(1)}, u32[]{:S(2)}, u32[]{:S(2)}) collective-permute-start(f32[2,1,128,128]{3,2,1,0:T(8,128)S(1)} %stack.77), channel_id=1, source_target_pairs={{0,128},{32,160},{64,192},{96,224},{128,0},{160,32},{192,64},{224,... | collective-permute-start | bytes 393224 | tf_op jit(solution)/shard_map/ppermute | solution.py:13
  182.1 6.5 collective-permute-start.27
  182.7 8.7 %collective-permute-start.28 = (f32[2,1,128,128]{3,2,0,1:T(8,128)S(1)}, f32[2,1,128,128]{3,2,0,1:T(8,128)S(1)}, u32[]{:S(2)}, u32[]{:S(2)}) collective-permute-start(f32[2,1,128,128]{3,2,0,1:T(8,128)S(1)} %get-tuple-element.81), channel_id=1, source_target_pairs={{0,64},{32,96},{64,0},{96,32},{128,192},{160,224},{192,128},{224,1... | collective-permute-start | bytes 393224 | tf_op jit(solution)/shard_map/ppermute | solution.py:13
  185.5 13.4 %collective-permute-start.3 = (f32[2,3,128,128]{3,2,1,0:T(8,128)S(1)}, f32[2,3,128,128]{3,2,1,0:T(8,128)S(1)}, u32[]{:S(2)}, u32[]{:S(2)}) collective-permute-start(f32[2,3,128,128]{3,2,1,0:T(8,128)S(1)} %get-tuple-element.51), channel_id=1, source_target_pairs={{0,64},{32,96},{64,0},{96,32},{128,192},{160,224},{192,128},{224,1... | collective-permute-start | bytes 1179656 | tf_op jit(solution)/shard_map/ppermute | solution.py:13
  186.1 17.0 %collective-permute-start.4 = (f32[2,3,128,128]{3,2,1,0:T(8,128)S(1)}, f32[2,3,128,128]{3,2,1,0:T(8,128)S(1)}, u32[]{:S(2)}, u32[]{:S(2)}) collective-permute-start(f32[2,3,128,128]{3,2,1,0:T(8,128)S(1)} %get-tuple-element.50), channel_id=1, source_target_pairs={{0,64},{32,96},{64,0},{96,32},{128,192},{160,224},{192,128},{224,1... | collective-permute-start | bytes 1179656 | tf_op jit(solution)/shard_map/ppermute | solution.py:13
  191.5 12.9 %collective-permute-start.29 = (f32[2,1,128,128]{3,2,0,1:T(8,128)S(1)}, f32[2,1,128,128]{3,2,0,1:T(8,128)S(1)}, u32[]{:S(2)}, u32[]{:S(2)}) collective-permute-start(f32[2,1,128,128]{3,2,0,1:T(8,128)S(1)} %get-tuple-element.78), channel_id=1, source_target_pairs={{0,32},{32,0},{64,96},{96,64},{128,160},{160,128},{192,224},{224,1... | collective-permute-start | bytes 393224 | tf_op jit(solution)/shard_map/ppermute | solution.py:13
  191.6 12.8 %collective-permute-start.30 = (f32[2,1,128,128]{3,2,0,1:T(8,128)S(1)}, f32[2,1,128,128]{3,2,0,1:T(8,128)S(1)}, u32[]{:S(2)}, u32[]{:S(2)}) collective-permute-start(f32[2,1,128,128]{3,2,0,1:T(8,128)S(1)} %get-tuple-element.79), channel_id=1, source_target_pairs={{0,32},{32,0},{64,96},{96,64},{128,160},{160,128},{192,224},{224,1... | collective-permute-start | bytes 393224 | tf_op jit(solution)/shard_map/ppermute | solution.py:13
  203.3 2.3 collective-permute-start.5
  203.4 2.3 collective-permute-start.6
  211.3 1.4 collective-permute-start.31
  213.1 6.5 collective-permute-start.33
  213.8 7.8 %collective-permute-start.34 = (f32[2,1,128,128]{3,2,1,0:T(8,128)S(1)}, f32[2,1,128,128]{3,2,1,0:T(8,128)S(1)}, u32[]{:S(2)}, u32[]{:S(2)}) collective-permute-start(f32[2,1,128,128]{3,2,1,0:T(8,128)S(1)} %get-tuple-element.74), channel_id=1, source_target_pairs={{0,64},{32,96},{64,0},{96,32},{128,192},{160,224},{192,128},{224,1... | collective-permute-start | bytes 393224 | tf_op jit(solution)/shard_map/ppermute | solution.py:13
  221.7 7.7 %collective-permute-start.35 = (f32[2,1,128,128]{3,2,1,0:T(8,128)S(1)}, f32[2,1,128,128]{3,2,1,0:T(8,128)S(1)}, u32[]{:S(2)}, u32[]{:S(2)}) collective-permute-start(f32[2,1,128,128]{3,2,1,0:T(8,128)S(1)} %get-tuple-element.72), channel_id=1, source_target_pairs={{0,128},{32,160},{64,192},{96,224},{128,0},{160,32},{192,64},{224,... | collective-permute-start | bytes 393224 | tf_op jit(solution)/shard_map/ppermute | solution.py:13
  222.1 8.8 %collective-permute-start.36 = (f32[2,1,128,128]{3,2,1,0:T(8,128)S(1)}, f32[2,1,128,128]{3,2,1,0:T(8,128)S(1)}, u32[]{:S(2)}, u32[]{:S(2)}) collective-permute-start(f32[2,1,128,128]{3,2,1,0:T(8,128)S(1)} %get-tuple-element.17), channel_id=1, source_target_pairs={{0,128},{32,160},{64,192},{96,224},{128,0},{160,32},{192,64},{224,... | collective-permute-start | bytes 393224 | tf_op jit(solution)/shard_map/ppermute | solution.py:13
  231.0 6.9 collective-permute-start.37
  232.1 7.2 collective-permute-start.38
  239.4 5.1 collective-permute-start.39
  240.7 5.2 collective-permute-start.40
  246.1 1.6 collective-permute-start.42
  251.1 1.4 collective-permute-start.7
  253.0 6.5 collective-permute-start.10
  254.2 7.3 collective-permute-start.9
  261.6 7.5 collective-permute-start.11
  264.0 6.9 collective-permute-start.12
  271.1 7.5 collective-permute-start.13
  273.4 6.7 collective-permute-start.14
  280.1 5.2 collective-permute-start.15
  281.4 5.3 collective-permute-start.16
  286.7 1.5 collective-permute-start.17
  286.9 1.8 collective-permute-start.18
  294.5 6.5 collective-permute-start.21
  295.8 7.3 collective-permute-start.22
  303.1 7.9 %collective-permute-start.23 = (f32[2,1,128,128]{3,2,0,1:T(8,128)S(1)}, f32[2,1,128,128]{3,2,0,1:T(8,128)S(1)}, u32[]{:S(2)}, u32[]{:S(2)}) collective-permute-start(f32[2,1,128,128]{3,2,0,1:T(8,128)S(1)} %get-tuple-element.64), channel_id=1, source_target_pairs={{0,128},{32,160},{64,192},{96,224},{128,0},{160,32},{192,64},{224,... | collective-permute-start | bytes 393224 | tf_op jit(solution)/shard_map/ppermute | solution.py:13
  305.1 7.4 collective-permute-start.24
  314.3 438.1 %reduce-scatter.5.cloned.1.call-start = ((), (), s32[]{:S(2)}) async-start(), calls=%async_computation.5 | async-start | bytes 2162688 | tf_op jit(solution)/shard_map/reduce_scatter | solution.py:212
  314.5 1.5 collective-permute-start.44
  316.1 6.5 collective-permute-start.45
  317.4 7.3 collective-permute-start.46
  324.8 7.9 %collective-permute-start.47 = (f32[2,1,128,128]{3,2,1,0:T(8,128)S(1)}, f32[2,1,128,128]{3,2,1,0:T(8,128)S(1)}, u32[]{:S(2)}, u32[]{:S(2)}) collective-permute-start(f32[2,1,128,128]{3,2,1,0:T(8,128)S(1)} %broadcast_multiply_fusion.4), channel_id=1, source_target_pairs={{0,128},{32,160},{64,192},{96,224},{128,0},{160,32},{192,64},{224,... | collective-permute-start | bytes 393224 | tf_op jit(solution)/shard_map/ppermute | solution.py:13
  326.6 7.5 collective-permute-start.48
  334.3 3.2 collective-permute-start.49
  (17 other events, 512.8 us)
Sparse Core Ops, SparseCore 0:
  10.4 73.5 all-gather.2
  86.5 69.6 all-gather.4
  314.5 217.2 reduce-scatter.2
  535.4 217.0 reduce-scatter.4
where the time goes:
time: 768 us; the launch traced here: 761 us
  waiting for transfers between devices  653 us (85%)
  starting transfers between devices  56.1 us (7%)
  matrix products  23.4 us (3%)
  between operations  15.8 us (2%)
    reduce_scatter x1, waiting for transfers between devices, on_device(): lax.psum_scatter(lax.dot_general(picked, grad_flat, (((1,), (1,)), ((), (...  219 us
    reduce_scatter x1, waiting for transfers between devices, on_device(): lax.psum_scatter(lax.dot_general(picked, second_order_output, (((0,), (1,...  192 us
    ppermute x48, waiting for transfers between devices, swapped(): return lax.ppermute(value, axis, pairs)  102 us
    all_gather x1, waiting for transfers between devices, on_device(): lax.all_gather(tokens, 'chan', axis=1, tiled=True)  70.3 us
    all_gather x1, waiting for transfers between devices, on_device(): lax.all_gather(cotangent, 'chan', axis=1, tiled=True)  66.9 us
    ppermute x48, starting transfers between devices, swapped(): return lax.ppermute(value, axis, pairs)  52.1 us
  transfers between devices with their start and end apart: 54, of which 47 were waited for; matrix products, arithmetic and copies ran while one was open for 2% of the time, Pallas kernels for 0%

commit v1 on v0

--- a/solution.py
+++ b/solution.py
@@ -179,7 +179,9 @@
         tiled=True,
     ).T.astype(jnp.bfloat16)
     grad_two = lax.dot_general(
-        lax.all_gather(cotangent, "chan", axis=1, tiled=True),
+        jnp.concatenate(
+            lax.all_to_all(jnp.stack([cotangent] * lax.axis_size("chan")), "chan", 0, 0), axis=1
+        ),
         out_weight,
         (((1,), (1,)), ((), ())),
         preferred_element_type=jnp.float32,

time: 768 us -> 711 us (0.926)
  waiting for transfers between devices: 653 us -> 582 us
  starting transfers between devices: 56.1 us -> 67.4 us
    all_gather x1 -> x0, waiting for transfers between devices: 66.9 us -> none  [on_device(): lax.all_gather(cotangent, 'chan', axis=1, tiled=True)]
    all_to_all x0 -> x1, starting transfers between devices: none -> 11.3 us  [on_device(): lax.all_to_all(jnp.stack([cotangent] * lax.axis_size('chan')), 'chan', 0, 0)]
    all_gather x1, waiting for transfers between devices: 70.3 us -> 60 us  [on_device(): lax.all_gather(tokens, 'chan', axis=1, tiled=True)]
  transfers between devices with their start and end apart: 54 -> 54, of which waited for: 47 -> 47; matrix products, arithmetic and copies ran while one was open for 2% -> 3% of each run, Pallas kernels for 0% -> 0%
where the time goes in v1:
time: 711 us; the launch traced here: 703 us
  waiting for transfers between devices  582 us (82%)
  starting transfers between devices  67.4 us (9%)
  matrix products  22.9 us (3%)
  between operations  15.7 us (2%)
  local copies, waits for them, and re-layouts  7.73 us (1%)
  other arithmetic  7.43 us (1%)
    reduce_scatter x1, waiting for transfers between devices, on_device(): lax.psum_scatter(lax.dot_general(picked, grad_flat, (((1,), (1,)), ((), (...  219 us
    reduce_scatter x1, waiting for transfers between devices, on_device(): lax.psum_scatter(lax.dot_general(picked, second_order_output, (((0,), (1,...  192 us
    ppermute x48, waiting for transfers between devices, swapped(): return lax.ppermute(value, axis, pairs)  106 us
    all_gather x1, waiting for transfers between devices, on_device(): lax.all_gather(tokens, 'chan', axis=1, tiled=True)  60 us
    ppermute x48, starting transfers between devices, swapped(): return lax.ppermute(value, axis, pairs)  52.1 us
  transfers between devices with their start and end apart: 54, of which 47 were waited for; matrix products, arithmetic and copies ran while one was open for 3% of the time, Pallas kernels for 0%

profile of v1, /device:TPU:8, one launch (start us, length us, event | category | flops | bytes accessed | tf_op | source)
XLA Modules:
  0.0 702.9 jit_solution(2248353483719122339)
XLA Ops:
  10.0 11.3 %all-to-all-start = ((bf16[32,128,128]{1,2,0:T(8,128)(2,1)}), bf16[32,128,128]{1,2,0:T(8,128)(2,1)S(1)}, u32[]{:S(2)}, u32[]{:S(2)}) async-start(bf16[32,128,128]{1,2,0:T(8,128)(2,1)} %stack.54), calls=%async_computation.1 | async-start | bytes 2097152 | tf_op jit(solution)/shard_map/all_to_all | solution.py:183
  21.6 4.8 copy.188
  26.4 60.0 %all-gather.2.cloned.1.call-done = bf16[128,4096]{1,0:T(8,128)(2,1)} async-done(((bf16[128,128]{1,0:T(8,128)(2,1)}), bf16[128,4096]{1,0:T(8,128)(2,1)}) %all-gather.2.cloned.1.call-update) | async-done | bytes 1048592 | tf_op jit(solution)/shard_map/all_gather | solution.py:142
  86.4 3.3 fusion.349
  89.7 1.9 collective-permute-start
  92.4 2.2 collective-permute-done
  94.8 2.2 collective-permute-start.1
  97.1 1.5 collective-permute-start.2
  98.6 2.2 collective-permute-start.25
  100.8 1.5 collective-permute-start.26
  102.7 16.8 %collective-permute-done.25 = f32[2,1,128,128]{3,2,1,0:T(8,128)S(1)} collective-permute-done((f32[2,1,128,128]{3,2,1,0:T(8,128)S(1)}, f32[2,1,128,128]{3,2,1,0:T(8,128)S(1)}, u32[]{:S(2)}, u32[]{:S(2)}) %collective-permute-start.25) | collective-permute-done | bytes 131104 | tf_op jit(solution)/shard_map/ppermute | solution.py:13
  121.6 1.5 collective-permute-start.28
  127.4 2.8 collective-permute-done.28
  130.8 7.8 %collective-permute-done.3 = f32[2,3,128,128]{3,2,1,0:T(8,128)S(1)} collective-permute-done((f32[2,3,128,128]{3,2,1,0:T(8,128)S(1)}, f32[2,3,128,128]{3,2,1,0:T(8,128)S(1)}, u32[]{:S(2)}, u32[]{:S(2)}) %collective-permute-start.3) | collective-permute-done | bytes 393248 | tf_op jit(solution)/shard_map/ppermute | solution.py:13
  138.6 6.0 collective-permute-done.4
  157.9 3.8 collective-permute-done.33
  161.7 2.0 collective-permute-done.34
  164.6 2.9 collective-permute-start.36
  167.5 4.1 collective-permute-done.35
  174.2 2.7 collective-permute-start.38
  176.9 3.2 collective-permute-done.37
  181.5 1.6 collective-permute-start.39
  183.9 2.6 collective-permute-done.39
  186.5 1.8 collective-permute-done.40
  197.6 4.3 collective-permute-done.10
  201.9 2.0 collective-permute-done.9
  204.0 2.1 collective-permute-start.11
  206.1 1.5 collective-permute-start.12
  207.7 4.2 collective-permute-done.11
  213.6 1.8 collective-permute-start.13
  215.5 1.9 collective-permute-start.14
  217.3 3.5 collective-permute-done.13
  225.0 2.3 collective-permute-done.15
  238.7 4.3 collective-permute-done.21
  243.0 2.0 collective-permute-done.22
  245.1 2.0 collective-permute-start.23
  247.2 1.6 collective-permute-start.24
  248.7 4.3 collective-permute-done.23
  254.7 1.7 convolution_bitcast_fusion.1
  260.3 4.3 collective-permute-done.45
  264.6 2.2 collective-permute-done.46
  266.9 1.8 collective-permute-start.47
  268.7 1.8 collective-permute-start.48
  270.5 4.3 collective-permute-done.47
  276.4 1.9 collective-permute-start.49
  279.6 2.5 convolution_bitcast_fusion
  282.1 191.7 %reduce-scatter.3.cloned.1.call-done = f32[128,128]{0,1:T(8,128)} async-done(((f32[4096,128]{0,1:T(8,128)}), f32[128,128]{0,1:T(8,128)}) %reduce-scatter.3.cloned.1.call-update) | async-done | bytes 65552 | tf_op jit(solution)/shard_map/reduce_scatter | solution.py:170
  475.2 219.4 %reduce-scatter.5.cloned.1.call-done = f32[128,128]{0,1:T(8,128)} async-done(((f32[4096,128]{0,1:T(8,128)}), f32[128,128]{0,1:T(8,128)}) %reduce-scatter.5.cloned.1.call-update) | async-done | bytes 65552 | tf_op jit(solution)/shard_map/reduce_scatter | solution.py:214
  (184 shorter events, 67.1 us)
Async XLA Ops:
  7.2 79.2 %all-gather.2.cloned.1.call-start = ((), (), s32[]{:S(2)}) async-start(), calls=%async_computation.3 | async-start | bytes 1081344 | tf_op jit(solution)/shard_map/all_gather | solution.py:142
  10.0 81.6 %all-to-all-start = ((bf16[32,128,128]{1,2,0:T(8,128)(2,1)}), bf16[32,128,128]{1,2,0:T(8,128)(2,1)S(1)}, u32[]{:S(2)}, u32[]{:S(2)}) async-start(bf16[32,128,128]{1,2,0:T(8,128)(2,1)} %stack.54), calls=%async_computation.1 | async-start | bytes 2097152 | tf_op jit(solution)/shard_map/all_to_all | solution.py:183
  21.4 452.4 %reduce-scatter.3.cloned.1.call-start = ((), (), s32[]{:S(2)}) async-start(), calls=%async_computation.4 | async-start | bytes 2162688 | tf_op jit(solution)/shard_map/reduce_scatter | solution.py:170
  89.7 4.9 collective-permute-start
  94.8 28.2 %collective-permute-start.1 = (f32[2,3,128,128]{3,2,1,0:T(8,128)S(1)}, f32[2,3,128,128]{3,2,1,0:T(8,128)}, u32[]{:S(2)}, u32[]{:S(2)}) collective-permute-start(f32[2,3,128,128]{3,2,1,0:T(8,128)S(1)} %pad_maximum_fusion), channel_id=1, source_target_pairs={{0,128},{32,160},{64,192},{96,224},{128,0},{160,32},{192,64},{224,... | collective-permute-start | bytes 1179656 | tf_op jit(solution)/shard_map/ppermute | solution.py:13
  97.1 26.0 %collective-permute-start.2 = (f32[2,3,128,128]{3,2,1,0:T(8,128)S(1)}, f32[2,3,128,128]{3,2,1,0:T(8,128)}, u32[]{:S(2)}, u32[]{:S(2)}) collective-permute-start(f32[2,3,128,128]{3,2,1,0:T(8,128)S(1)} %stack.51), channel_id=1, source_target_pairs={{0,128},{32,160},{64,192},{96,224},{128,0},{160,32},{192,64},{224,... | collective-permute-start | bytes 1179656 | tf_op jit(solution)/shard_map/ppermute | solution.py:13
  98.6 20.8 %collective-permute-start.25 = (f32[2,1,128,128]{3,2,1,0:T(8,128)S(1)}, f32[2,1,128,128]{3,2,1,0:T(8,128)S(1)}, u32[]{:S(2)}, u32[]{:S(2)}) collective-permute-start(f32[2,1,128,128]{3,2,1,0:T(8,128)S(1)} %pad_maximum_fusion.6), channel_id=1, source_target_pairs={{0,128},{32,160},{64,192},{96,224},{128,0},{160,32},{192,64},{224,... | collective-permute-start | bytes 393224 | tf_op jit(solution)/shard_map/ppermute | solution.py:13
  100.8 20.0 %collective-permute-start.26 = (f32[2,1,128,128]{3,2,1,0:T(8,128)S(1)}, f32[2,1,128,128]{3,2,1,0:T(8,128)S(1)}, u32[]{:S(2)}, u32[]{:S(2)}) collective-permute-start(f32[2,1,128,128]{3,2,1,0:T(8,128)S(1)} %stack.113), channel_id=1, source_target_pairs={{0,128},{32,160},{64,192},{96,224},{128,0},{160,32},{192,64},{224,... | collective-permute-start | bytes 393224 | tf_op jit(solution)/shard_map/ppermute | solution.py:13
  120.9 6.5 collective-permute-start.27
  121.6 8.6 %collective-permute-start.28 = (f32[2,1,128,128]{3,2,0,1:T(8,128)S(1)}, f32[2,1,128,128]{3,2,0,1:T(8,128)S(1)}, u32[]{:S(2)}, u32[]{:S(2)}) collective-permute-start(f32[2,1,128,128]{3,2,0,1:T(8,128)S(1)} %get-tuple-element.81), channel_id=1, source_target_pairs={{0,64},{32,96},{64,0},{96,32},{128,192},{160,224},{192,128},{224,1... | collective-permute-start | bytes 393224 | tf_op jit(solution)/shard_map/ppermute | solution.py:13
  124.3 14.3 %collective-permute-start.3 = (f32[2,3,128,128]{3,2,1,0:T(8,128)S(1)}, f32[2,3,128,128]{3,2,1,0:T(8,128)S(1)}, u32[]{:S(2)}, u32[]{:S(2)}) collective-permute-start(f32[2,3,128,128]{3,2,1,0:T(8,128)S(1)} %get-tuple-element.51), channel_id=1, source_target_pairs={{0,64},{32,96},{64,0},{96,32},{128,192},{160,224},{192,128},{224,1... | collective-permute-start | bytes 1179656 | tf_op jit(solution)/shard_map/ppermute | solution.py:13
  125.0 19.7 %collective-permute-start.4 = (f32[2,3,128,128]{3,2,1,0:T(8,128)S(1)}, f32[2,3,128,128]{3,2,1,0:T(8,128)S(1)}, u32[]{:S(2)}, u32[]{:S(2)}) collective-permute-start(f32[2,3,128,128]{3,2,1,0:T(8,128)S(1)} %get-tuple-element.50), channel_id=1, source_target_pairs={{0,64},{32,96},{64,0},{96,32},{128,192},{160,224},{192,128},{224,1... | collective-permute-start | bytes 1179656 | tf_op jit(solution)/shard_map/ppermute | solution.py:13
  130.3 15.6 %collective-permute-start.29 = (f32[2,1,128,128]{3,2,0,1:T(8,128)S(1)}, f32[2,1,128,128]{3,2,0,1:T(8,128)S(1)}, u32[]{:S(2)}, u32[]{:S(2)}) collective-permute-start(f32[2,1,128,128]{3,2,0,1:T(8,128)S(1)} %get-tuple-element.78), channel_id=1, source_target_pairs={{0,32},{32,0},{64,96},{96,64},{128,160},{160,128},{192,224},{224,1... | collective-permute-start | bytes 393224 | tf_op jit(solution)/shard_map/ppermute | solution.py:13
  130.4 15.5 %collective-permute-start.30 = (f32[2,1,128,128]{3,2,0,1:T(8,128)S(1)}, f32[2,1,128,128]{3,2,0,1:T(8,128)S(1)}, u32[]{:S(2)}, u32[]{:S(2)}) collective-permute-start(f32[2,1,128,128]{3,2,0,1:T(8,128)S(1)} %get-tuple-element.79), channel_id=1, source_target_pairs={{0,32},{32,0},{64,96},{96,64},{128,160},{160,128},{192,224},{224,1... | collective-permute-start | bytes 393224 | tf_op jit(solution)/shard_map/ppermute | solution.py:13
  144.8 2.3 collective-permute-start.5
  144.9 2.3 collective-permute-start.6
  153.4 1.4 collective-permute-start.31
  155.3 6.5 collective-permute-start.33
  156.4 7.3 %collective-permute-start.34 = (f32[2,1,128,128]{3,2,1,0:T(8,128)S(1)}, f32[2,1,128,128]{3,2,1,0:T(8,128)S(1)}, u32[]{:S(2)}, u32[]{:S(2)}) collective-permute-start(f32[2,1,128,128]{3,2,1,0:T(8,128)S(1)} %get-tuple-element.74), channel_id=1, source_target_pairs={{0,64},{32,96},{64,0},{96,32},{128,192},{160,224},{192,128},{224,1... | collective-permute-start | bytes 393224 | tf_op jit(solution)/shard_map/ppermute | solution.py:13
  163.8 7.7 %collective-permute-start.35 = (f32[2,1,128,128]{3,2,1,0:T(8,128)S(1)}, f32[2,1,128,128]{3,2,1,0:T(8,128)S(1)}, u32[]{:S(2)}, u32[]{:S(2)}) collective-permute-start(f32[2,1,128,128]{3,2,1,0:T(8,128)S(1)} %get-tuple-element.72), channel_id=1, source_target_pairs={{0,128},{32,160},{64,192},{96,224},{128,0},{160,32},{192,64},{224,... | collective-permute-start | bytes 393224 | tf_op jit(solution)/shard_map/ppermute | solution.py:13
  164.6 8.4 %collective-permute-start.36 = (f32[2,1,128,128]{3,2,1,0:T(8,128)S(1)}, f32[2,1,128,128]{3,2,1,0:T(8,128)S(1)}, u32[]{:S(2)}, u32[]{:S(2)}) collective-permute-start(f32[2,1,128,128]{3,2,1,0:T(8,128)S(1)} %get-tuple-element.17), channel_id=1, source_target_pairs={{0,128},{32,160},{64,192},{96,224},{128,0},{160,32},{192,64},{224,... | collective-permute-start | bytes 393224 | tf_op jit(solution)/shard_map/ppermute | solution.py:13
  173.1 6.9 collective-permute-start.37
  174.2 7.2 %collective-permute-start.38 = (f32[2,1,128,128]{3,2,0,1:T(8,128)S(1)}, f32[2,1,128,128]{3,2,0,1:T(8,128)S(1)}, u32[]{:S(2)}, u32[]{:S(2)}) collective-permute-start(f32[2,1,128,128]{3,2,0,1:T(8,128)S(1)} %pad_bitcast_fusion), channel_id=1, source_target_pairs={{0,128},{32,160},{64,192},{96,224},{128,0},{160,32},{192,64},{224,... | collective-permute-start | bytes 393224 | tf_op jit(solution)/shard_map/ppermute | solution.py:13
  181.5 5.1 collective-permute-start.39
  183.1 5.2 collective-permute-start.40
  188.5 1.6 collective-permute-start.42
  193.6 1.4 collective-permute-start.7
  195.5 6.5 collective-permute-start.10
  196.6 7.3 %collective-permute-start.9 = (f32[2,1,128,128]{3,2,0,1:T(8,128)S(1)}, f32[2,1,128,128]{3,2,0,1:T(8,128)S(1)}, u32[]{:S(2)}, u32[]{:S(2)}) collective-permute-start(f32[2,1,128,128]{3,2,0,1:T(8,128)S(1)} %get-tuple-element.41), channel_id=1, source_target_pairs={{0,64},{32,96},{64,0},{96,32},{128,192},{160,224},{192,128},{224,1... | collective-permute-start | bytes 393224 | tf_op jit(solution)/shard_map/ppermute | solution.py:13
  204.0 7.9 %collective-permute-start.11 = (f32[2,1,128,128]{3,2,0,1:T(8,128)S(1)}, f32[2,1,128,128]{3,2,0,1:T(8,128)S(1)}, u32[]{:S(2)}, u32[]{:S(2)}) collective-permute-start(f32[2,1,128,128]{3,2,0,1:T(8,128)S(1)} %get-tuple-element.68), channel_id=1, source_target_pairs={{0,128},{32,160},{64,192},{96,224},{128,0},{160,32},{192,64},{224,... | collective-permute-start | bytes 393224 | tf_op jit(solution)/shard_map/ppermute | solution.py:13
  206.1 7.3 %collective-permute-start.12 = (f32[2,1,128,128]{3,2,0,1:T(8,128)S(1)}, f32[2,1,128,128]{3,2,0,1:T(8,128)S(1)}, u32[]{:S(2)}, u32[]{:S(2)}) collective-permute-start(f32[2,1,128,128]{3,2,0,1:T(8,128)S(1)} %get-tuple-element.39), channel_id=1, source_target_pairs={{0,128},{32,160},{64,192},{96,224},{128,0},{160,32},{192,64},{224,... | collective-permute-start | bytes 393224 | tf_op jit(solution)/shard_map/ppermute | solution.py:13
  213.6 7.2 %collective-permute-start.13 = (f32[2,1,128,128]{3,2,0,1:T(8,128)S(1)}, f32[2,1,128,128]{3,2,0,1:T(8,128)S(1)}, u32[]{:S(2)}, u32[]{:S(2)}) collective-permute-start(f32[2,1,128,128]{3,2,0,1:T(8,128)S(1)} %pad_maximum_fusion.5), channel_id=1, source_target_pairs={{0,128},{32,160},{64,192},{96,224},{128,0},{160,32},{192,64},{224,... | collective-permute-start | bytes 393224 | tf_op jit(solution)/shard_map/ppermute | solution.py:13
  215.5 6.7 collective-permute-start.14
  222.2 5.1 collective-permute-start.15
  223.6 5.1 collective-permute-start.16
  228.7 1.5 collective-permute-start.17
  228.9 1.8 collective-permute-start.18
  236.5 6.5 collective-permute-start.21
  237.9 7.1 %collective-permute-start.22 = (f32[2,1,128,128]{3,2,0,1:T(8,128)S(1)}, f32[2,1,128,128]{3,2,0,1:T(8,128)S(1)}, u32[]{:S(2)}, u32[]{:S(2)}) collective-permute-start(f32[2,1,128,128]{3,2,0,1:T(8,128)S(1)} %get-tuple-element.66), channel_id=1, source_target_pairs={{0,64},{32,96},{64,0},{96,32},{128,192},{160,224},{192,128},{224,1... | collective-permute-start | bytes 393224 | tf_op jit(solution)/shard_map/ppermute | solution.py:13
  245.1 7.9 %collective-permute-start.23 = (f32[2,1,128,128]{3,2,0,1:T(8,128)S(1)}, f32[2,1,128,128]{3,2,0,1:T(8,128)S(1)}, u32[]{:S(2)}, u32[]{:S(2)}) collective-permute-start(f32[2,1,128,128]{3,2,0,1:T(8,128)S(1)} %get-tuple-element.64), channel_id=1, source_target_pairs={{0,128},{32,160},{64,192},{96,224},{128,0},{160,32},{192,64},{224,... | collective-permute-start | bytes 393224 | tf_op jit(solution)/shard_map/ppermute | solution.py:13
  247.2 7.3 %collective-permute-start.24 = (f32[2,1,128,128]{3,2,0,1:T(8,128)S(1)}, f32[2,1,128,128]{3,2,0,1:T(8,128)S(1)}, u32[]{:S(2)}, u32[]{:S(2)}) collective-permute-start(f32[2,1,128,128]{3,2,0,1:T(8,128)S(1)} %get-tuple-element.29), channel_id=1, source_target_pairs={{0,128},{32,160},{64,192},{96,224},{128,0},{160,32},{192,64},{224,... | collective-permute-start | bytes 393224 | tf_op jit(solution)/shard_map/ppermute | solution.py:13
  256.4 438.2 %reduce-scatter.5.cloned.1.call-start = ((), (), s32[]{:S(2)}) async-start(), calls=%async_computation.5 | async-start | bytes 2162688 | tf_op jit(solution)/shard_map/reduce_scatter | solution.py:214
  256.6 1.5 collective-permute-start.44
  258.2 6.5 collective-permute-start.45
  259.5 7.3 %collective-permute-start.46 = (f32[2,1,128,128]{3,2,1,0:T(8,128)S(1)}, f32[2,1,128,128]{3,2,1,0:T(8,128)S(1)}, u32[]{:S(2)}, u32[]{:S(2)}) collective-permute-start(f32[2,1,128,128]{3,2,1,0:T(8,128)S(1)} %get-tuple-element.62), channel_id=1, source_target_pairs={{0,64},{32,96},{64,0},{96,32},{128,192},{160,224},{192,128},{224,1... | collective-permute-start | bytes 393224 | tf_op jit(solution)/shard_map/ppermute | solution.py:13
  266.9 7.9 %collective-permute-start.47 = (f32[2,1,128,128]{3,2,1,0:T(8,128)S(1)}, f32[2,1,128,128]{3,2,1,0:T(8,128)S(1)}, u32[]{:S(2)}, u32[]{:S(2)}) collective-permute-start(f32[2,1,128,128]{3,2,1,0:T(8,128)S(1)} %broadcast_multiply_fusion.4), channel_id=1, source_target_pairs={{0,128},{32,160},{64,192},{96,224},{128,0},{160,32},{192,64},{224,... | collective-permute-start | bytes 393224 | tf_op jit(solution)/shard_map/ppermute | solution.py:13
  268.7 7.5 %collective-permute-start.48 = (f32[2,1,128,128]{3,2,1,0:T(8,128)S(1)}, f32[2,1,128,128]{3,2,1,0:T(8,128)S(1)}, u32[]{:S(2)}, u32[]{:S(2)}) collective-permute-start(f32[2,1,128,128]{3,2,1,0:T(8,128)S(1)} %get-tuple-element.60), channel_id=1, source_target_pairs={{0,128},{32,160},{64,192},{96,224},{128,0},{160,32},{192,64},{224,... | collective-permute-start | bytes 393224 | tf_op jit(solution)/shard_map/ppermute | solution.py:13
  276.4 3.2 collective-permute-start.49
  (15 other events, 261.7 us)
Sparse Core Ops, SparseCore 0:
  10.4 75.9 all-gather.1
  256.5 217.2 reduce-scatter.2
  477.6 216.9 reduce-scatter.4
